TPU v7x, 32 devices: a whole 2x2x4 slice. The times are simulated.
32 devices in a mesh: dp: 4 (over x, core), fsdp: 8 (over z, y).
Axes of the slice: x: 2, y: 2, z: 4, core: 2. Of those that a mesh axis runs over, the one named last changes fastest.
Arguments:
- tokens: bfloat16 [2, 4096, 1024], P(None, ('dp', 'fsdp')), may hold values from -6 to 6
- scene_ids: int32 [2, 4, 1024], P(None, 'dp', 'fsdp'), may hold values from 0 to 1, never falling along the last dimension, each value on 1 to 682 neighbouring positions
- w_qkv: bfloat16 [1024, 3072], P(('dp', 'fsdp')), may hold values from -0.1875 to 0.1875
- w_out: bfloat16 [1024, 1024], P(('dp', 'fsdp')), may hold values from -6 to 6
- w_up: bfloat16 [1024, 4096], P(('dp', 'fsdp')), may hold values from -0.1875 to 0.1875
- w_down: bfloat16 [4096, 1024], P(('dp', 'fsdp')), may hold values from -0.09375 to 0.09375
- gain_one: bfloat16 [1024], P(('dp', 'fsdp')), may hold values from 0.5 to 1.5
- bias_one: bfloat16 [1024], P(('dp', 'fsdp')), may hold values from -1 to 1
- gain_two: bfloat16 [1024], P(('dp', 'fsdp')), may hold values from 0.5 to 1.5
- bias_two: bfloat16 [1024], P(('dp', 'fsdp')), may hold values from -1 to 1
- cotangent: bfloat16 [2, 4096, 1024], P(None, ('dp', 'fsdp')), may hold values from -6 to 6
Outputs:
- output: bfloat16 [2, 4096, 1024], P(None, ('dp', 'fsdp'))
- input_grad: float32 [2, 4096, 1024], P(None, ('dp', 'fsdp'))
- grad_qkv: float32 [1024, 3072], P(('dp', 'fsdp'))
- grad_out: float32 [1024, 1024], P(('dp', 'fsdp'))
- grad_up: float32 [1024, 4096], P(('dp', 'fsdp'))
- grad_down: float32 [4096, 1024], P(('dp', 'fsdp'))
- grad_gain_one: float32 [1024], P(('dp', 'fsdp'))
- grad_bias_one: float32 [1024], P(('dp', 'fsdp'))
- grad_gain_two: float32 [1024], P(('dp', 'fsdp'))
- grad_bias_two: float32 [1024], P(('dp', 'fsdp'))
Inputs may be any that keep to these rules, and one draw needn't show every extreme that they name: `scene_ids`: in each scene group of a micro-batch the scene numbers never fall, each of the 2 scenes holds 1 to 682 tokens.
All inputs are finite; a program needn't handle non-finite values.
Results may differ from a plain program's by a relative error of at most 0.012.
Values may be sent and summed in bfloat16 or wider, within the bound.
No kernel may reach another device: no remote copies, remote signals or barrier semaphores. Data moves between devices by JAX's collectives and lax.ppermute only.
A program may use at most 320 MiB of HBM per device.

v0:
```python
import math
import jax
import jax.numpy as jnp
from jax import lax
from jax.sharding import PartitionSpec as P

HEAD_DIM = 64
eps_norm = 1e-05
lowest_score = -1000000000.0


def layer_norm(values, gain, shift):
    average = jnp.mean(values, axis=-1, keepdims=True)
    centered = values - average
    variance = jnp.mean(centered * centered, axis=-1, keepdims=True)
    return centered * lax.rsqrt(variance + eps_norm) * gain + shift


def exact_gelu(values):
    return jax.nn.gelu(values, approximate=False)


def key_blocks(kv_all, key_scene):
    total = kv_all.shape[0]
    size = 512
    return (
        kv_all.reshape(total // size, size, kv_all.shape[1]),
        key_scene.reshape(total // size, size),
    )


def block_scores(queries, block, scenes, own_scene):
    scale = 1.0 / math.sqrt(HEAD_DIM)
    width = block.shape[1] // 2
    key_heads = block[:, :width].reshape(block.shape[0], -1, HEAD_DIM)
    scores = (
        jnp.einsum("qhd,khd->hqk", queries, key_heads, preferred_element_type=jnp.float32) * scale
    )
    same_scene = own_scene[:, None] == scenes[None, :]
    return jnp.where(same_scene[None], scores, lowest_score)


def block_values(block):
    width = block.shape[1] // 2
    return block[:, width:].reshape(block.shape[0], -1, HEAD_DIM)


def attention_forward(query_cols, kv_all, own_scene, key_scene):
    row_count = query_cols.shape[0]
    queries = query_cols.reshape(row_count, -1, HEAD_DIM)
    head_count = queries.shape[1]
    blocks, scenes = key_blocks(kv_all, key_scene)

    def peak_step(carry, item):
        peak, total = carry
        masked = block_scores(queries, item[0], item[1], own_scene)
        new_peak = jnp.maximum(peak, jnp.max(masked, axis=-1, keepdims=True))
        total = total * jnp.exp(peak - new_peak) + jnp.sum(
            jnp.exp(masked - new_peak), axis=-1, keepdims=True
        )
        return ((new_peak, total), None)

    start = (
        jnp.full((head_count, row_count, 1), -jnp.inf, jnp.float32),
        jnp.zeros((head_count, row_count, 1), jnp.float32),
    )
    (peak, total), unused = lax.scan(peak_step, start, (blocks, scenes))
    log_total = peak + jnp.log(total)

    def mix_step(accum, item):
        masked = block_scores(queries, item[0], item[1], own_scene)
        probs = jnp.exp(masked - log_total).astype(jnp.bfloat16)
        return (
            accum
            + jnp.einsum(
                "hqk,khd->qhd", probs, block_values(item[0]), preferred_element_type=jnp.float32
            ),
            None,
        )

    mixed, unused = lax.scan(
        mix_step, jnp.zeros((row_count, head_count, HEAD_DIM), jnp.float32), (blocks, scenes)
    )
    return (mixed.reshape(row_count, -1).astype(jnp.bfloat16), log_total)


def attention_backward(query_cols, kv_all, own_scene, key_scene, log_total, grad_mixed):
    scale = 1.0 / math.sqrt(HEAD_DIM)
    row_count = query_cols.shape[0]
    queries = query_cols.reshape(row_count, -1, HEAD_DIM)
    head_count = queries.shape[1]
    grad_heads = grad_mixed.reshape(row_count, -1, HEAD_DIM)
    blocks, scenes = key_blocks(kv_all, key_scene)

    def inner_step(inner, item):
        masked = block_scores(queries, item[0], item[1], own_scene)
        probs = jnp.exp(masked - log_total)
        grad_probs = jnp.einsum(
            "qhd,khd->hqk", grad_heads, block_values(item[0]), preferred_element_type=jnp.float32
        )
        return (inner + jnp.sum(probs * grad_probs, axis=-1, keepdims=True), None)

    inner, unused = lax.scan(
        inner_step, jnp.zeros((head_count, row_count, 1), jnp.float32), (blocks, scenes)
    )

    def grad_step(grad_queries, item):
        block = item[0]
        width = block.shape[1] // 2
        key_heads = block[:, :width].reshape(block.shape[0], -1, HEAD_DIM)
        masked = block_scores(queries, block, item[1], own_scene)
        probs = jnp.exp(masked - log_total)
        grad_probs = jnp.einsum(
            "qhd,khd->hqk", grad_heads, block_values(block), preferred_element_type=jnp.float32
        )
        grad_scores = (probs * (grad_probs - inner)).astype(jnp.bfloat16)
        grad_queries = (
            grad_queries
            + jnp.einsum("hqk,khd->qhd", grad_scores, key_heads, preferred_element_type=jnp.float32)
            * scale
        )
        grad_keys = (
            jnp.einsum("hqk,qhd->khd", grad_scores, queries, preferred_element_type=jnp.float32)
            * scale
        )
        grad_values = jnp.einsum(
            "hqk,qhd->khd",
            probs.astype(jnp.bfloat16),
            grad_heads,
            preferred_element_type=jnp.float32,
        )
        both = jnp.concatenate(
            [grad_keys.reshape(block.shape[0], -1), grad_values.reshape(block.shape[0], -1)], axis=1
        )
        return (grad_queries, both)

    grad_queries, grad_pairs = lax.scan(
        grad_step, jnp.zeros((row_count, head_count, HEAD_DIM), jnp.float32), (blocks, scenes)
    )
    return (grad_queries.reshape(row_count, -1), grad_pairs.reshape(kv_all.shape[0], -1))


def outer_sum(left, right):
    return jnp.einsum("ti,tj->ij", left, right, preferred_element_type=jnp.float32)


def back_product(grad_rows, weight):
    return jnp.einsum("tj,ij->ti", grad_rows, weight, preferred_element_type=jnp.float32)


def body(
    tokens, scene_ids, w_qkv, w_out, w_up, w_down, gain_one, bias_one, gain_two, bias_two, cotangent
):
    micro_count = tokens.shape[0]
    all_scenes = lax.all_gather(scene_ids, "fsdp", axis=2, tiled=True)
    totals = (
        jnp.zeros(w_qkv.shape, jnp.float32),
        jnp.zeros(w_out.shape, jnp.float32),
        jnp.zeros(w_up.shape, jnp.float32),
        jnp.zeros(w_down.shape, jnp.float32),
        jnp.zeros(gain_one.shape, jnp.float32),
        jnp.zeros(bias_one.shape, jnp.float32),
        jnp.zeros(gain_two.shape, jnp.float32),
        jnp.zeros(bias_two.shape, jnp.float32),
    )
    results = []
    input_grads = []
    for batch_index in range(micro_count):
        forward_weights = (
            lax.all_gather(w_qkv, ("dp", "fsdp"), axis=0, tiled=True),
            lax.all_gather(w_out, ("dp", "fsdp"), axis=0, tiled=True),
            lax.all_gather(w_up, ("dp", "fsdp"), axis=0, tiled=True),
            lax.all_gather(w_down, ("dp", "fsdp"), axis=0, tiled=True),
            lax.all_gather(gain_one, ("dp", "fsdp"), axis=0, tiled=True),
            lax.all_gather(bias_one, ("dp", "fsdp"), axis=0, tiled=True),
            lax.all_gather(gain_two, ("dp", "fsdp"), axis=0, tiled=True),
            lax.all_gather(bias_two, ("dp", "fsdp"), axis=0, tiled=True),
        )
        full_qkv, full_out, full_up, full_down, full_gone, full_bone, full_gtwo, full_btwo = (
            forward_weights
        )
        width = full_qkv.shape[1] // 3
        block_tokens = tokens[batch_index].astype(jnp.float32)
        own_scene = scene_ids[batch_index, 0]
        key_scene = all_scenes[batch_index, 0]
        normed_one, pull_one = jax.vjp(
            layer_norm, block_tokens, full_gone.astype(jnp.float32), full_bone.astype(jnp.float32)
        )
        normed_one_low = normed_one.astype(jnp.bfloat16)
        projected = jnp.dot(normed_one_low, full_qkv, preferred_element_type=jnp.float32).astype(
            jnp.bfloat16
        )
        query_cols = projected[:, :width]
        kv_all = lax.all_gather(projected[:, width:], "fsdp", axis=0, tiled=True)
        mixed_low, log_total = attention_forward(query_cols, kv_all, own_scene, key_scene)
        hidden = block_tokens + jnp.dot(mixed_low, full_out, preferred_element_type=jnp.float32)
        normed_two, pull_two = jax.vjp(
            layer_norm, hidden, full_gtwo.astype(jnp.float32), full_btwo.astype(jnp.float32)
        )
        normed_two_low = normed_two.astype(jnp.bfloat16)
        upward = jnp.dot(normed_two_low, full_up, preferred_element_type=jnp.float32)
        activated, pull_gelu = jax.vjp(exact_gelu, upward)
        activated_low = activated.astype(jnp.bfloat16)
        result = hidden + jnp.dot(activated_low, full_down, preferred_element_type=jnp.float32)
        results.append(result.astype(jnp.bfloat16))
        backward_weights = (
            lax.all_gather(w_qkv, ("dp", "fsdp"), axis=0, tiled=True),
            lax.all_gather(w_out, ("dp", "fsdp"), axis=0, tiled=True),
            lax.all_gather(w_up, ("dp", "fsdp"), axis=0, tiled=True),
            lax.all_gather(w_down, ("dp", "fsdp"), axis=0, tiled=True),
            lax.all_gather(gain_one, ("dp", "fsdp"), axis=0, tiled=True),
            lax.all_gather(bias_one, ("dp", "fsdp"), axis=0, tiled=True),
            lax.all_gather(gain_two, ("dp", "fsdp"), axis=0, tiled=True),
            lax.all_gather(bias_two, ("dp", "fsdp"), axis=0, tiled=True),
        )
        back_qkv, back_out, back_up, back_down = (
            backward_weights[0],
            backward_weights[1],
            backward_weights[2],
            backward_weights[3],
        )
        grad_result = cotangent[batch_index].astype(jnp.float32)
        grad_result_low = grad_result.astype(jnp.bfloat16)
        local_down = outer_sum(activated_low, grad_result_low)
        grad_act = back_product(grad_result_low, back_down)
        grad_upward = pull_gelu(grad_act)[0].astype(jnp.bfloat16)
        local_up = outer_sum(normed_two_low, grad_upward)
        grad_norm_two = back_product(grad_upward, back_up)
        grad_hidden_part, local_gtwo, local_btwo = pull_two(grad_norm_two)
        grad_hidden = grad_result + grad_hidden_part
        grad_hidden_low = grad_hidden.astype(jnp.bfloat16)
        local_out = outer_sum(mixed_low, grad_hidden_low)
        grad_mixed = back_product(grad_hidden_low, back_out).astype(jnp.bfloat16)
        grad_queries, grad_pairs = attention_backward(
            query_cols, kv_all, own_scene, key_scene, log_total, grad_mixed
        )
        grad_own_pairs = lax.psum_scatter(
            grad_pairs.astype(jnp.bfloat16), "fsdp", scatter_dimension=0, tiled=True
        ).astype(jnp.float32)
        grad_projected = jnp.concatenate([grad_queries, grad_own_pairs], axis=1).astype(
            jnp.bfloat16
        )
        local_qkv = outer_sum(normed_one_low, grad_projected)
        grad_norm_one = back_product(grad_projected, back_qkv)
        grad_token_part, local_gone, local_bone = pull_one(grad_norm_one)
        input_grads.append(grad_hidden + grad_token_part)
        summed = (
            lax.psum_scatter(local_qkv, ("dp", "fsdp"), scatter_dimension=0, tiled=True),
            lax.psum_scatter(local_out, ("dp", "fsdp"), scatter_dimension=0, tiled=True),
            lax.psum_scatter(local_up, ("dp", "fsdp"), scatter_dimension=0, tiled=True),
            lax.psum_scatter(local_down, ("dp", "fsdp"), scatter_dimension=0, tiled=True),
            lax.psum_scatter(local_gone, ("dp", "fsdp"), scatter_dimension=0, tiled=True),
            lax.psum_scatter(local_bone, ("dp", "fsdp"), scatter_dimension=0, tiled=True),
            lax.psum_scatter(local_gtwo, ("dp", "fsdp"), scatter_dimension=0, tiled=True),
            lax.psum_scatter(local_btwo, ("dp", "fsdp"), scatter_dimension=0, tiled=True),
        )
        totals = jax.tree.map(jnp.add, totals, tuple(summed))
    output = jnp.stack(results, axis=0)
    input_grad = jnp.stack(input_grads, axis=0)
    return (
        output,
        input_grad,
        totals[0],
        totals[1],
        totals[2],
        totals[3],
        totals[4],
        totals[5],
        totals[6],
        totals[7],
    )


def solution(mesh):
    return jax.shard_map(
        body,
        mesh=mesh,
        in_specs=(
            P(None, ("dp", "fsdp"), None),
            P(None, "dp", "fsdp"),
            P(("dp", "fsdp"), None),
            P(("dp", "fsdp"), None),
            P(("dp", "fsdp"), None),
            P(("dp", "fsdp"), None),
            P(("dp", "fsdp")),
            P(("dp", "fsdp")),
            P(("dp", "fsdp")),
            P(("dp", "fsdp")),
            P(None, ("dp", "fsdp"), None),
        ),
        out_specs=(
            P(None, ("dp", "fsdp"), None),
            P(None, ("dp", "fsdp"), None),
            P(("dp", "fsdp"), None),
            P(("dp", "fsdp"), None),
            P(("dp", "fsdp"), None),
            P(("dp", "fsdp"), None),
            P(("dp", "fsdp")),
            P(("dp", "fsdp")),
            P(("dp", "fsdp")),
            P(("dp", "fsdp")),
        ),
        check_vma=False,
    )
```

profile of v0, /device:TPU:0, one launch (start us, length us, event | category | flops | bytes accessed | tf_op | source)
XLA Modules:
  0.0 1742.1 jit_solution(13039055786084457197)
XLA Ops:
  11.3 42.4 %all-reduce.9 = (bf16[1024]{0:T(1024)(128)(2,1)S(1)}, bf16[1024]{0:T(1024)(128)(2,1)S(1)}, bf16[1024]{0:T(1024)(128)(2,1)S(1)}, bf16[1024]{0:T(1024)(128)(2,1)S(1)}) all-reduce(bf16[1024]{0:T(1024)(128)(2,1)S(1)} %dynamic-update-slice.1, bf16[1024]{0:T(1024)(128)(2,1)S(1)} %dynamic-update-slice, ...), channel_id=1, replica_groups=mesh['dp'=4,'fsdp'=8] {'dp','fsdp'}, use_global_device_ids=true, to_apply=%add.1 | all-reduce | flops 4096 | bytes 16384
  56.3 26.9 %all-gather.7.cloned.1.call-done = bf16[1024,3072]{1,0:T(8,128)(2,1)} async-done(((bf16[32,3072]{1,0:T(8,128)(2,1)}), bf16[1024,3072]{1,0:T(8,128)(2,1)}) %all-gather.7.cloned.1.call-update) | async-done | bytes 6291472 | tf_op jit(solution)/shard_map/all_gather | solution.py:170
  94.9 19.6 %all_gather.26 = s32[2,1,1024]{2,1,0:T(1,128)S(1)} all-gather(s32[2,1,128]{2,1,0:T(1,128)S(1)} %copy-done.82), channel_id=1, replica_groups=mesh['dp'=4,'fsdp'=8] {'fsdp'}, dimensions={2}, use_global_device_ids=true | all-gather | bytes 9216 | tf_op jit(solution)/shard_map/all_gather | solution.py:155
  115.0 45.2 %all-gather.17.cloned.1.call-done = bf16[1024,2048]{1,0:T(8,128)(2,1)} async-done(((bf16[128,2048]{1,0:T(8,128)(2,1)}), bf16[1024,2048]{1,0:T(8,128)(2,1)}) %all-gather.17.cloned.1.call-update) | async-done | bytes 4194320 | tf_op jit(solution)/shard_map/all_gather | solution.py:194
  166.5 15.9 while.98
  182.4 10.1 while.99
  193.7 40.9 %all-gather.9.cloned.1.call-done = bf16[1024,2048]{1,0:T(8,128)(2,1)} async-done(((bf16[128,2048]{1,0:T(8,128)(2,1)}), bf16[1024,2048]{1,0:T(8,128)(2,1)}) %all-gather.9.cloned.1.call-update) | async-done | bytes 4194320 | tf_op jit(solution)/shard_map/all_gather | solution.py:194
  240.8 16.0 while.96
  256.9 10.2 while.97
  268.2 24.1 %all-gather.11.cloned.1.call-done = bf16[1024,1024]{1,0:T(8,128)(2,1)} async-done(((bf16[32,1024]{1,0:T(8,128)(2,1)}), bf16[1024,1024]{1,0:T(8,128)(2,1)}) %all-gather.11.cloned.1.call-update) | async-done | bytes 2097168 | tf_op jit(solution)/shard_map/all_gather | solution.py:171
  295.6 75.8 %all-gather.13.cloned.1.call-done = bf16[1024,4096]{1,0:T(8,128)(2,1)} async-done(((bf16[32,4096]{1,0:T(8,128)(2,1)}), bf16[1024,4096]{1,0:T(8,128)(2,1)}) %all-gather.13.cloned.1.call-update) | async-done | bytes 8388624 | tf_op jit(solution)/shard_map/all_gather | solution.py:172
  380.3 69.9 %all-gather.15.cloned.1.call-done = bf16[4096,1024]{1,0:T(8,128)(2,1)} async-done(((bf16[128,1024]{1,0:T(8,128)(2,1)}), bf16[4096,1024]{1,0:T(8,128)(2,1)}) %all-gather.15.cloned.1.call-update) | async-done | bytes 8388624 | tf_op jit(solution)/shard_map/all_gather | solution.py:173
  450.3 10.1 add_convert_fusion
  467.2 7.6 add_convert_fusion.1
  483.3 8.9 while.100
  494.7 34.5 %while.101 = (s32[]{:T(128)}, f32[128,16,64]{0,2,1:T(8,128)}, bf16[2,512,2048]{2,1,0:T(8,128)(2,1)}, bf16[2,512,2048]{1,2,0:T(8,128)(2,1)}, s32[1,1,128]{2,1,0:T...) while((s32[]{:T(128)}, f32[128,16,64]{0,2,1:T(8,128)}, ...), condition=%wide.region_26.27_spmd.clone, body=%wide.region_25.26_spmd.clone.sunk | while | flops 687276032 | bytes 83065600 | solution.py:137
  530.2 11.2 while.102
  543.9 34.3 %while.103 = (s32[]{:T(128)}, f32[128,16,64]{0,2,1:T(8,128)}, bf16[2,512,2048]{2,1,0:T(8,128)(2,1)}, bf16[2,512,2048]{1,2,0:T(8,128)(2,1)}, s32[1,1,128]{2,1,0:T...) while((s32[]{:T(128)}, f32[128,16,64]{0,2,1:T(8,128)}, ...), condition=%wide.region_36.37_spmd.clone, body=%wide.region_35.36_spmd.clone.sunk | while | flops 687276032 | bytes 80968392 | solution.py:137
  584.2 31.9 %reduce-scatter.7.cloned.1.call-done = bf16[128,2048]{1,0:T(8,128)(2,1)} async-done(((bf16[1024,2048]{1,0:T(8,128)(2,1)}), bf16[128,2048]{1,0:T(8,128)(2,1)}) %reduce-scatter.7.cloned.1.call-update) | async-done | bytes 524304 | tf_op jit(solution)/shard_map/reduce_scatter | solution.py:237
  616.1 7.5 fusion.95
  623.6 84.4 %reduce-scatter.9.cloned.1.call-done = bf16[128,2048]{1,0:T(8,128)(2,1)} async-done(((bf16[1024,2048]{1,0:T(8,128)(2,1)}), bf16[128,2048]{1,0:T(8,128)(2,1)}) %reduce-scatter.9.cloned.1.call-update) | async-done | bytes 524304 | tf_op jit(solution)/shard_map/reduce_scatter | solution.py:237
  708.0 11.2 convolution_add_fusion.2
  724.0 8.3 convolution_add_fusion.1
  733.3 11.1 fusion.104
  744.4 13.3 convolution_add_fusion
  758.5 9.6 fusion.68
  768.1 8.3 fusion.69
  782.5 42.9 %all-reduce.8 = (f32[1024]{0:T(1024)S(1)}, f32[1024]{0:T(1024)S(1)}, f32[1024]{0:T(1024)S(1)}, f32[1024]{0:T(1024)S(1)}) all-reduce(f32[1024]{0:T(1024)S(1)} %add.238, f32[1024]{0:T(1024)S(1)} %add.239, f32[1024]{0:T(1024)S(1)} %add.240, f32[1024]{0:T(1024)S(1)} %add.241), channel_id=16, replica_groups=mesh['dp'=4,'fsdp'=8] {'dp','fsdp'}, use_global_device_ids=true, to_apply=%region_49.50.clone | all-reduce | flops 4096 | bytes 32768
  829.3 25.3 %reduce-scatter.13.cloned.1.call-done = f32[32,1024]{1,0:T(8,128)} async-done(((f32[1024,1024]{1,0:T(8,128)}), f32[32,1024]{1,0:T(8,128)}) %reduce-scatter.13.cloned.1.call-update) | async-done | bytes 131088 | tf_op jit(solution)/shard_map/reduce_scatter | solution.py:249
  854.6 160.0 %reduce-scatter.11.cloned.1.call-done = f32[32,3072]{1,0:T(8,128)} async-done(((f32[1024,3072]{1,0:T(8,128)}), f32[32,3072]{1,0:T(8,128)}) %reduce-scatter.11.cloned.1.call-update) | async-done | bytes 393232 | tf_op jit(solution)/shard_map/reduce_scatter | solution.py:248
  1014.6 360.2 %reduce-scatter.15.cloned.1.call-done = f32[32,4096]{1,0:T(8,128)} async-done(((f32[1024,4096]{1,0:T(8,128)}), f32[32,4096]{1,0:T(8,128)}) %reduce-scatter.15.cloned.1.call-update) | async-done | bytes 524304 | tf_op jit(solution)/shard_map/reduce_scatter | solution.py:250
  1374.8 360.2 %reduce-scatter.17.cloned.1.call-done = f32[128,1024]{1,0:T(8,128)} async-done(((f32[4096,1024]{1,0:T(8,128)}), f32[128,1024]{1,0:T(8,128)}) %reduce-scatter.17.cloned.1.call-update) | async-done | bytes 524304 | tf_op jit(solution)/shard_map/reduce_scatter | solution.py:251
  (456 shorter events, 228.1 us)
Async XLA Ops:
  7.2 76.1 %all-gather.7.cloned.1.call-start = ((), (), s32[]{:S(2)}) async-start(), calls=%async_computation.6 | async-start | bytes 6488064 | tf_op jit(solution)/shard_map/all_gather | solution.py:170
  7.9 152.3 %all-gather.17.cloned.1.call-start = ((), (), s32[]{:S(2)}) async-start(), calls=%async_computation.11 | async-start | bytes 4718592 | tf_op jit(solution)/shard_map/all_gather | solution.py:194
  88.1 146.5 %all-gather.9.cloned.1.call-start = ((), (), s32[]{:S(2)}) async-start(), calls=%async_computation.7 | async-start | bytes 4718592 | tf_op jit(solution)/shard_map/all_gather | solution.py:194
  93.0 199.3 %all-gather.11.cloned.1.call-start = ((), (), s32[]{:S(2)}) async-start(), calls=%async_computation.8 | async-start | bytes 2162688 | tf_op jit(solution)/shard_map/all_gather | solution.py:171
  93.5 277.9 %all-gather.13.cloned.1.call-start = ((), (), s32[]{:S(2)}) async-start(), calls=%async_computation.9 | async-start | bytes 8650752 | tf_op jit(solution)/shard_map/all_gather | solution.py:172
  94.1 356.1 %all-gather.15.cloned.1.call-start = ((), (), s32[]{:S(2)}) async-start(), calls=%async_computation.10 | async-start | bytes 8650752 | tf_op jit(solution)/shard_map/all_gather | solution.py:173
  94.7 521.4 %reduce-scatter.7.cloned.1.call-start = ((), (), s32[]{:S(2)}) async-start(), calls=%async_computation.12 | async-start | bytes 4718592 | tf_op jit(solution)/shard_map/reduce_scatter | solution.py:237
  114.5 263.1 %copy-start.45 = (f32[1024]{0:T(1024)}, f32[1024]{0:T(1024)S(1)}, u32[]{:S(2)}) copy-start(f32[1024]{0:T(1024)S(1)} %convert_element_type.139) | copy-start | bytes 12292
  114.6 363.9 %copy-start.41 = (f32[1024]{0:T(1024)}, f32[1024]{0:T(1024)S(1)}, u32[]{:S(2)}) copy-start(f32[1024]{0:T(1024)S(1)} %convert_element_type.138) | copy-start | bytes 12292
  192.5 48.3 %copy-start.1 = (bf16[128,16,64]{0,2,1:T(8,128)(2,1)}, bf16[128,16,64]{0,2,1:T(8,128)(2,1)S(1)}, u32[]{:S(2)}) copy-start(bf16[128,16,64]{0,2,1:T(8,128)(2,1)S(1)} %get-tuple-element.1718) | copy-start | bytes 786436
  192.5 48.3 %copy-start.50 = (s32[2,512]{1,0:T(2,128)}, s32[2,512]{1,0:T(2,128)S(1)}, u32[]{:S(2)}) copy-start(s32[2,512]{1,0:T(2,128)S(1)} %get-tuple-element.1743) | copy-start | bytes 12292
  192.5 48.3 %copy-start.54 = (s32[1,1,128]{2,1,0:T(1,128)}, s32[1,1,128]{2,1,0:T(1,128)S(1)}, u32[]{:S(2)}) copy-start(s32[1,1,128]{2,1,0:T(1,128)S(1)} %get-tuple-element.1754) | copy-start | bytes 1540
  192.5 48.3 %copy-start.80 = (f32[16,128,1]{1,0,2:T(8,128)}, f32[16,128,1]{1,0,2:T(8,128)S(1)}, u32[]{:S(2)}) copy-start(f32[16,128,1]{1,0,2:T(8,128)S(1)} %get-tuple-element.1763) | copy-start | bytes 24580
  193.7 98.6 %copy-start.24 = (bf16[128,16,64]{0,2,1:T(8,128)(2,1)}, bf16[128,16,64]{0,2,1:T(8,128)(2,1)S(1)}, u32[]{:S(2)}) copy-start(bf16[128,16,64]{0,2,1:T(8,128)(2,1)S(1)} %convert_element_type.147) | copy-start | bytes 786436
  294.6 183.9 %copy-start.11 = (f32[128,1024]{1,0:T(8,128)}, f32[128,1024]{1,0:T(8,128)S(1)}, u32[]{:S(2)}) copy-start(f32[128,1024]{1,0:T(8,128)S(1)} %get-tuple-element.1024) | copy-start | bytes 1572868
  294.6 183.9 %copy-start.63 = (f32[128]{0:T(128)}, f32[128]{0:T(128)S(1)}, u32[]{:S(2)}) copy-start(f32[128]{0:T(128)S(1)} %broadcast_multiply_fusion) | copy-start | bytes 1540
  295.4 183.1 %copy-start.13 = (f32[128,1024]{1,0:T(8,128)}, f32[128,1024]{1,0:T(8,128)S(1)}, u32[]{:S(2)}) copy-start(f32[128,1024]{1,0:T(8,128)S(1)} %get-tuple-element.1026) | copy-start | bytes 1572868
  295.4 183.1 %copy-start.65 = (f32[128]{0:T(128)}, f32[128]{0:T(128)S(1)}, u32[]{:S(2)}) copy-start(f32[128]{0:T(128)S(1)} %broadcast_multiply_fusion.2) | copy-start | bytes 1540
  295.6 182.9 %copy-start.72 = (f32[128]{0:T(128)}, f32[128]{0:T(128)S(1)}, u32[]{:S(2)}) copy-start(f32[128]{0:T(128)S(1)} %fusion.117) | copy-start | bytes 1540
  295.6 182.9 %copy-start.74 = (f32[128]{0:T(128)}, f32[128]{0:T(128)S(1)}, u32[]{:S(2)}) copy-start(f32[128]{0:T(128)S(1)} %fusion.115) | copy-start | bytes 1540
  377.6 72.7 %copy-start.33 = (bf16[2,128,1024]{2,1,0:T(8,128)(2,1)S(1)}, bf16[2,128,1024]{2,1,0:T(8,128)(2,1)}, u32[]{:S(2)}) copy-start(bf16[2,128,1024]{2,1,0:T(8,128)(2,1)} %param.37) | copy-start | bytes 1572868
  529.3 178.7 %reduce-scatter.9.cloned.1.call-start = ((), (), s32[]{:S(2)}) async-start(), calls=%async_computation.13 | async-start | bytes 4718592 | tf_op jit(solution)/shard_map/reduce_scatter | solution.py:237
  578.2 276.5 %reduce-scatter.13.cloned.1.call-start = ((), (), s32[]{:S(2)}) async-start(), calls=%async_computation.15 | async-start | bytes 4325376 | tf_op jit(solution)/shard_map/reduce_scatter | solution.py:249
  582.8 431.8 %reduce-scatter.11.cloned.1.call-start = ((), (), s32[]{:S(2)}) async-start(), calls=%async_computation.14 | async-start | bytes 12976128 | tf_op jit(solution)/shard_map/reduce_scatter | solution.py:248
  584.2 123.9 %copy-start.59 = (f32[128]{0:T(128)S(1)}, f32[128]{0:T(128)}, u32[]{:S(2)}) copy-start(f32[128]{0:T(128)} %copy-done.58) | copy-start | bytes 1540
  584.2 123.8 %copy-start.68 = (f32[128]{0:T(128)S(1)}, f32[128]{0:T(128)}, u32[]{:S(2)}) copy-start(f32[128]{0:T(128)} %copy-done.67) | copy-start | bytes 1540
  719.3 655.5 %reduce-scatter.15.cloned.1.call-start = ((), (), s32[]{:S(2)}) async-start(), calls=%async_computation.16 | async-start | bytes 17301504 | tf_op jit(solution)/shard_map/reduce_scatter | solution.py:250
  732.3 1002.7 %reduce-scatter.17.cloned.1.call-start = ((), (), s32[]{:S(2)}) async-start(), calls=%async_computation.17 | async-start | bytes 17301504 | tf_op jit(solution)/shard_map/reduce_scatter | solution.py:251
  779.6 48.2 %copy-start.18 = (f32[128,1024]{1,0:T(8,128)S(1)}, f32[128,1024]{1,0:T(8,128)}, u32[]{:S(2)}) copy-start(f32[128,1024]{1,0:T(8,128)} %copy-done.17) | copy-start | bytes 1572868
  779.6 48.2 %copy-start.20 = (f32[128,1024]{1,0:T(8,128)S(1)}, f32[128,1024]{1,0:T(8,128)}, u32[]{:S(2)}) copy-start(f32[128,1024]{1,0:T(8,128)} %copy-done.19) | copy-start | bytes 1572868
  779.6 48.2 %copy-start.84 = (f32[128]{0:T(128)S(1)}, f32[128]{0:T(128)}, u32[]{:S(2)}) copy-start(f32[128]{0:T(128)} %copy-done.83) | copy-start | bytes 1540
  779.6 48.2 %copy-start.86 = (f32[128]{0:T(128)S(1)}, f32[128]{0:T(128)}, u32[]{:S(2)}) copy-start(f32[128]{0:T(128)} %copy-done.85) | copy-start | bytes 1540
  (82 other events, 720.9 us)
Sparse Core Ops, SparseCore 0:
  10.9 72.2 all-gather.6
  88.2 71.9 all-gather.16
  162.9 71.6 all-gather.8
  237.5 54.7 all-gather.10
  295.1 76.2 all-gather.12
  374.2 75.9 all-gather.14
  529.4 86.6 reduce-scatter.6
  620.2 87.8 reduce-scatter.8
  710.9 143.7 reduce-scatter.12
  861.1 153.4 reduce-scatter.10
  1017.6 357.1 reduce-scatter.14
  1377.6 357.3 reduce-scatter.16
where the time goes:
time: 1750 us; the launch traced here: 1740 us
  waiting for transfers between devices  1310 us (75%)
  matrix products  199 us (11%)
  blocking collectives  105 us (6%)
  local copies, waits for them, and re-layouts  82.9 us (5%)
  other arithmetic  29.3 us (2%)
    reduce_scatter x1, waiting for transfers between devices, body(): lax.psum_scatter(local_up, ('dp', 'fsdp'), scatter_dimension=0, tiled=True)  360 us
    reduce_scatter x1, waiting for transfers between devices, body(): lax.psum_scatter(local_down, ('dp', 'fsdp'), scatter_dimension=0, tiled=T...  360 us
    reduce_scatter x1, waiting for transfers between devices, body(): lax.psum_scatter(local_qkv, ('dp', 'fsdp'), scatter_dimension=0, tiled=True)  160 us
    reduce_scatter x2, waiting for transfers between devices, body(): lax.psum_scatter(grad_pairs.astype(jnp.bfloat16), 'fsdp', scatter_dimensi...  116 us
    all_gather x2, waiting for transfers between devices, body(): kv_all = lax.all_gather(projected[:, width:], 'fsdp', axis=0, tiled=True)  86.2 us
    unnamed x2, blocking collectives  85.3 us
    all_gather x1, waiting for transfers between devices, body(): lax.all_gather(w_up, ('dp', 'fsdp'), axis=0, tiled=True)  75.8 us
    all_gather x1, waiting for transfers between devices, body(): lax.all_gather(w_down, ('dp', 'fsdp'), axis=0, tiled=True)  69.9 us
  transfers between devices with their start and end apart: 12, of which 12 were waited for; matrix products, arithmetic and copies ran while one was open for 13% of the time, Pallas kernels for 0%

commit v1 on v0

--- a/solution.py
+++ b/solution.py
@@ -191,7 +191,25 @@
             jnp.bfloat16
         )
         query_cols = projected[:, :width]
-        kv_all = lax.all_gather(projected[:, width:], "fsdp", axis=0, tiled=True)
+        value = projected[:, width:]
+        size_2, index, width_2 = (lax.axis_size("fsdp"), lax.axis_index("fsdp"), value.shape[0])
+        upward_2 = [(i, (i + 1) % size_2) for i in range(size_2)]
+        left_2 = [(i, (i - 1) % size_2) for i in range(size_2)]
+        out = jnp.zeros((*value.shape[:0], size_2 * width_2, *value.shape[0 + 1 :]), value.dtype)
+        out = lax.dynamic_update_slice_in_dim(out, value, index * width_2, axis=0)
+        from_left = from_right = value
+        half = size_2 // 2
+        for turn in range(1, half + 1):
+            from_left = lax.ppermute(from_left, "fsdp", upward_2)
+            out = lax.dynamic_update_slice_in_dim(
+                out, from_left, (index - turn) % size_2 * width_2, axis=0
+            )
+            if turn < size_2 - half:
+                from_right = lax.ppermute(from_right, "fsdp", left_2)
+                out = lax.dynamic_update_slice_in_dim(
+                    out, from_right, (index + turn) % size_2 * width_2, axis=0
+                )
+        kv_all = out
         mixed_low, log_total = attention_forward(query_cols, kv_all, own_scene, key_scene)
         hidden = block_tokens + jnp.dot(mixed_low, full_out, preferred_element_type=jnp.float32)
         normed_two, pull_two = jax.vjp(

time: 1750 us -> 1670 us (0.954)
  waiting for transfers between devices: 1310 us -> 1170 us
  local copies, waits for them, and re-layouts: 82.9 us -> 105 us
  starting transfers between devices: 0.86 us -> 21.1 us
  blocking collectives: 105 us -> 123 us
    ppermute x0 -> x14, waiting for transfers between devices: none -> 117 us  [the longest x6 97.6 us: body(): from_right = lax.ppermute(from_right, 'fsdp', left_2)]
    all_gather x2 -> x0, waiting for transfers between devices: 86.2 us -> none  [body(): kv_all = lax.all_gather(projected[:, width:], 'fsdp', axis=0, tiled=True)]
    all_gather x1, waiting for transfers between devices: 75.8 us -> 0.02 us  [body(): lax.all_gather(w_up, ('dp', 'fsdp'), axis=0, tiled=True)]
    all_gather x1, waiting for transfers between devices: 69.9 us -> 5.15 us  [body(): lax.all_gather(w_down, ('dp', 'fsdp'), axis=0, tiled=True)]
    all_gather x1, waiting for transfers between devices: 24.1 us -> 0.02 us  [body(): lax.all_gather(w_out, ('dp', 'fsdp'), axis=0, tiled=True)]
    all_gather x1, blocking collectives: 19.6 us -> 39.9 us  [body(): all_scenes = lax.all_gather(scene_ids, 'fsdp', axis=2, tiled=True)]
    ppermute x0 -> x14, starting transfers between devices: none -> 20.1 us  [the longest x8 11.2 us: body(): from_left = lax.ppermute(from_left, 'fsdp', upward_2)]
    dynamic_update_slice x0 -> x14, local copies, waits for them, and re-layouts: none -> 18.1 us  [the longest x8 11 us: body(): lax.dynamic_update_slice_in_dim(out, from_left, (index - turn) % size_2 *...]
  transfers between devices with their start and end apart: 12 -> 24, of which waited for: 12 -> 14; matrix products, arithmetic and copies ran while one was open for 13% -> 15% of each run, Pallas kernels for 0% -> 0%
where the time goes in v1:
time: 1670 us
  waiting for transfers between devices  1170 us (70%)
  matrix products  197 us (12%)
  blocking collectives  123 us (7%)
  local copies, waits for them, and re-layouts  105 us (6%)
  other arithmetic  29.3 us (2%)
  starting transfers between devices  21.1 us (1%)
    reduce_scatter x1, waiting for transfers between devices, body(): lax.psum_scatter(local_up, ('dp', 'fsdp'), scatter_dimension=0, tiled=True)  360 us
    reduce_scatter x1, waiting for transfers between devices, body(): lax.psum_scatter(local_down, ('dp', 'fsdp'), scatter_dimension=0, tiled=T...  360 us
    reduce_scatter x1, waiting for transfers between devices, body(): lax.psum_scatter(local_qkv, ('dp', 'fsdp'), scatter_dimension=0, tiled=True)  160 us
    reduce_scatter x2, waiting for transfers between devices, body(): lax.psum_scatter(grad_pairs.astype(jnp.bfloat16), 'fsdp', scatter_dimensi...  116 us
    ppermute x6, waiting for transfers between devices, body(): from_right = lax.ppermute(from_right, 'fsdp', left_2)  97.6 us
    unnamed x2, blocking collectives  83.6 us
    dot_general x8, matrix products, outer_sum(): jnp.einsum('ti,tj->ij', left, right, preferred_element_type=jnp.float32)  58.6 us
    all_gather x1, blocking collectives, body(): all_scenes = lax.all_gather(scene_ids, 'fsdp', axis=2, tiled=True)  39.9 us
  transfers between devices with their start and end apart: 24, of which 14 were waited for; matrix products, arithmetic and copies ran while one was open for 15% of the time, Pallas kernels for 0%

profile of v1, /device:TPU:0, one launch (start us, length us, event | category | flops | bytes accessed | tf_op | source)
XLA Modules:
  0.0 1665.8 jit_solution(3837942153092849710)
XLA Ops:
  12.8 42.3 %all-reduce.9 = (bf16[1024]{0:T(1024)(128)(2,1)S(1)}, bf16[1024]{0:T(1024)(128)(2,1)S(1)}, bf16[1024]{0:T(1024)(128)(2,1)S(1)}, bf16[1024]{0:T(1024)(128)(2,1)S(1)}) all-reduce(bf16[1024]{0:T(1024)(128)(2,1)S(1)} %dynamic-update-slice.1, bf16[1024]{0:T(1024)(128)(2,1)S(1)} %dynamic-update-slice, ...), channel_id=1, replica_groups=mesh['dp'=4,'fsdp'=8] {'dp','fsdp'}, use_global_device_ids=true, to_apply=%add.1 | all-reduce | flops 4096 | bytes 16384
  58.3 25.1 %all-gather.5.cloned.1.call-done = bf16[1024,3072]{1,0:T(8,128)(2,1)} async-done(((bf16[32,3072]{1,0:T(8,128)(2,1)}), bf16[1024,3072]{1,0:T(8,128)(2,1)}) %all-gather.5.cloned.1.call-update) | async-done | bytes 6291472 | tf_op jit(solution)/shard_map/all_gather | solution.py:170
  98.5 39.9 %all_gather.21 = s32[2,1,1024]{2,1,0:T(1,128)S(1)} all-gather(s32[2,1,128]{2,1,0:T(1,128)S(1)} %copy-done.84), channel_id=1, replica_groups=mesh['dp'=4,'fsdp'=8] {'fsdp'}, dimensions={2}, use_global_device_ids=true | all-gather | bytes 9216 | tf_op jit(solution)/shard_map/all_gather | solution.py:155
  149.2 30.5 %collective-permute-done.1 = bf16[128,2048]{1,0:T(8,128)(2,1)} collective-permute-done((bf16[128,2048]{1,0:T(8,128)(2,1)}, bf16[128,2048]{1,0:T(8,128)(2,1)}, u32[]{:S(2)}, u32[]{:S(2)}) %collective-permute-start.1) | collective-permute-done | bytes 524320 | tf_op jit(solution)/shard_map/ppermute | solution.py:208
  185.5 18.4 %collective-permute-done.10 = bf16[128,2048]{1,0:T(8,128)(2,1)S(1)} collective-permute-done((bf16[128,2048]{1,0:T(8,128)(2,1)}, bf16[128,2048]{1,0:T(8,128)(2,1)S(1)}, u32[]{:S(2)}, u32[]{:S(2)}) %collective-permute-start.10) | collective-permute-done | bytes 524320 | tf_op jit(solution)/shard_map/ppermute | solution.py:208
  208.6 21.6 %collective-permute-done.3 = bf16[128,2048]{1,0:T(8,128)(2,1)S(1)} collective-permute-done((bf16[128,2048]{1,0:T(8,128)(2,1)}, bf16[128,2048]{1,0:T(8,128)(2,1)S(1)}, u32[]{:S(2)}, u32[]{:S(2)}) %collective-permute-start.3) | collective-permute-done | bytes 524320 | tf_op jit(solution)/shard_map/ppermute | solution.py:208
  233.9 19.0 %collective-permute-done.4 = bf16[128,2048]{1,0:T(8,128)(2,1)} collective-permute-done((bf16[128,2048]{1,0:T(8,128)(2,1)S(1)}, bf16[128,2048]{1,0:T(8,128)(2,1)}, u32[]{:S(2)}, u32[]{:S(2)}) %collective-permute-start.4) | collective-permute-done | bytes 524320 | tf_op jit(solution)/shard_map/ppermute | solution.py:203
  259.2 27.0 %collective-permute-done.5 = bf16[128,2048]{1,0:T(8,128)(2,1)S(1)} collective-permute-done((bf16[128,2048]{1,0:T(8,128)(2,1)S(1)}, bf16[128,2048]{1,0:T(8,128)(2,1)S(1)}, u32[]{:S(2)}, u32[]{:S(2)}) %collective-permute-start.5) | collective-permute-done | bytes 524320 | tf_op jit(solution)/shard_map/ppermute | solution.py:208
  294.1 16.0 while.98
  310.1 10.1 while.99
  329.7 16.1 while.96
  345.7 10.3 while.97
  374.8 10.1 add_convert_fusion
  391.8 7.8 add_convert_fusion.1
  408.0 8.9 while.100
  419.4 34.4 %while.101 = (s32[]{:T(128)}, f32[128,16,64]{0,2,1:T(8,128)}, bf16[2,512,2048]{2,1,0:T(8,128)(2,1)}, bf16[2,512,2048]{1,2,0:T(8,128)(2,1)}, s32[1,1,128]{2,1,0:T...) while((s32[]{:T(128)}, f32[128,16,64]{0,2,1:T(8,128)}, ...), condition=%wide.region_26.27_spmd.clone, body=%wide.region_25.26_spmd.clone.sunk | while | flops 687276032 | bytes 83065600 | solution.py:137
  454.8 10.9 while.102
  468.3 34.3 %while.103 = (s32[]{:T(128)}, f32[128,16,64]{0,2,1:T(8,128)}, bf16[2,512,2048]{2,1,0:T(8,128)(2,1)}, bf16[2,512,2048]{1,2,0:T(8,128)(2,1)}, s32[1,1,128]{2,1,0:T...) while((s32[]{:T(128)}, f32[128,16,64]{0,2,1:T(8,128)}, ...), condition=%wide.region_36.37_spmd.clone, body=%wide.region_35.36_spmd.clone.sunk | while | flops 687276032 | bytes 80968392 | solution.py:137
  508.6 32.0 %reduce-scatter.7.cloned.1.call-done = bf16[128,2048]{1,0:T(8,128)(2,1)} async-done(((bf16[1024,2048]{1,0:T(8,128)(2,1)}), bf16[128,2048]{1,0:T(8,128)(2,1)}) %reduce-scatter.7.cloned.1.call-update) | async-done | bytes 524304 | tf_op jit(solution)/shard_map/reduce_scatter | solution.py:255
  540.6 7.5 fusion.95
  548.1 84.1 %reduce-scatter.9.cloned.1.call-done = bf16[128,2048]{1,0:T(8,128)(2,1)} async-done(((bf16[1024,2048]{1,0:T(8,128)(2,1)}), bf16[128,2048]{1,0:T(8,128)(2,1)}) %reduce-scatter.9.cloned.1.call-update) | async-done | bytes 524304 | tf_op jit(solution)/shard_map/reduce_scatter | solution.py:255
  632.2 11.2 convolution_add_fusion.2
  648.2 8.3 convolution_add_fusion.1
  657.5 11.2 fusion.104
  668.7 13.3 convolution_add_fusion
  682.8 9.6 fusion.68
  692.4 8.2 fusion.69
  706.8 41.3 %all-reduce.8 = (f32[1024]{0:T(1024)S(1)}, f32[1024]{0:T(1024)S(1)}, f32[1024]{0:T(1024)S(1)}, f32[1024]{0:T(1024)S(1)}) all-reduce(f32[1024]{0:T(1024)S(1)} %add.333, f32[1024]{0:T(1024)S(1)} %add.334, f32[1024]{0:T(1024)S(1)} %add.335, f32[1024]{0:T(1024)S(1)} %add.336), channel_id=16, replica_groups=mesh['dp'=4,'fsdp'=8] {'dp','fsdp'}, use_global_device_ids=true, to_apply=%region_49.50.clone | all-reduce | flops 4096 | bytes 32768
  751.9 26.8 %reduce-scatter.13.cloned.1.call-done = f32[32,1024]{1,0:T(8,128)} async-done(((f32[1024,1024]{1,0:T(8,128)}), f32[32,1024]{1,0:T(8,128)}) %reduce-scatter.13.cloned.1.call-update) | async-done | bytes 131088 | tf_op jit(solution)/shard_map/reduce_scatter | solution.py:267
  778.8 159.6 %reduce-scatter.11.cloned.1.call-done = f32[32,3072]{1,0:T(8,128)} async-done(((f32[1024,3072]{1,0:T(8,128)}), f32[32,3072]{1,0:T(8,128)}) %reduce-scatter.11.cloned.1.call-update) | async-done | bytes 393232 | tf_op jit(solution)/shard_map/reduce_scatter | solution.py:266
  938.4 360.2 %reduce-scatter.15.cloned.1.call-done = f32[32,4096]{1,0:T(8,128)} async-done(((f32[1024,4096]{1,0:T(8,128)}), f32[32,4096]{1,0:T(8,128)}) %reduce-scatter.15.cloned.1.call-update) | async-done | bytes 524304 | tf_op jit(solution)/shard_map/reduce_scatter | solution.py:268
  1298.6 360.2 %reduce-scatter.17.cloned.1.call-done = f32[128,1024]{1,0:T(8,128)} async-done(((f32[4096,1024]{1,0:T(8,128)}), f32[128,1024]{1,0:T(8,128)}) %reduce-scatter.17.cloned.1.call-update) | async-done | bytes 524304 | tf_op jit(solution)/shard_map/reduce_scatter | solution.py:269
  (498 shorter events, 273.3 us)
Async XLA Ops:
  7.2 76.1 %all-gather.5.cloned.1.call-start = ((), (), s32[]{:S(2)}) async-start(), calls=%async_computation.6 | async-start | bytes 6488064 | tf_op jit(solution)/shard_map/all_gather | solution.py:170
  7.9 349.2 %all-gather.7.cloned.1.call-start = ((), (), s32[]{:S(2)}) async-start(), calls=%async_computation.7 | async-start | bytes 2162688 | tf_op jit(solution)/shard_map/all_gather | solution.py:171
  8.7 351.9 %all-gather.9.cloned.1.call-start = ((), (), s32[]{:S(2)}) async-start(), calls=%async_computation.8 | async-start | bytes 8650752 | tf_op jit(solution)/shard_map/all_gather | solution.py:172
  9.4 365.4 %all-gather.11.cloned.1.call-start = ((), (), s32[]{:S(2)}) async-start(), calls=%async_computation.9 | async-start | bytes 8650752 | tf_op jit(solution)/shard_map/all_gather | solution.py:173
  88.9 51.7 %collective-permute-start.7 = (bf16[128,2048]{1,0:T(8,128)(2,1)}, bf16[128,2048]{1,0:T(8,128)(2,1)}, u32[]{:S(2)}, u32[]{:S(2)}) collective-permute-start(bf16[128,2048]{1,0:T(8,128)(2,1)} %get-tuple-element.1002), channel_id=1, source_target_pairs={{0,1},{1,2},{2,3},{3,4},{4,5},{5,6},{6,7},{7,0},{8,9},{9,10},{10,1... | collective-permute-start | bytes 1572872 | tf_op jit(solution)/shard_map/ppermute | solution.py:203
  90.4 50.8 %collective-permute-start.8 = (bf16[128,2048]{1,0:T(8,128)(2,1)}, bf16[128,2048]{1,0:T(8,128)(2,1)}, u32[]{:S(2)}, u32[]{:S(2)}) collective-permute-start(bf16[128,2048]{1,0:T(8,128)(2,1)} %get-tuple-element.1002), channel_id=1, source_target_pairs={{0,7},{1,0},{2,1},{3,2},{4,3},{5,4},{6,5},{7,6},{8,15},{9,8},{10,9... | collective-permute-start | bytes 1572872 | tf_op jit(solution)/shard_map/ppermute | solution.py:208
  98.4 47.0 %collective-permute-start = (bf16[128,2048]{1,0:T(8,128)(2,1)}, bf16[128,2048]{1,0:T(8,128)(2,1)}, u32[]{:S(2)}, u32[]{:S(2)}) collective-permute-start(bf16[128,2048]{1,0:T(8,128)(2,1)} %get-tuple-element.1000), channel_id=1, source_target_pairs={{0,1},{1,2},{2,3},{3,4},{4,5},{5,6},{6,7},{7,0},{8,9},{9,10},{10,1... | collective-permute-start | bytes 1572872 | tf_op jit(solution)/shard_map/ppermute | solution.py:203
  98.4 442.2 %reduce-scatter.7.cloned.1.call-start = ((), (), s32[]{:S(2)}) async-start(), calls=%async_computation.10 | async-start | bytes 4718592 | tf_op jit(solution)/shard_map/reduce_scatter | solution.py:255
  138.4 41.3 %collective-permute-start.1 = (bf16[128,2048]{1,0:T(8,128)(2,1)}, bf16[128,2048]{1,0:T(8,128)(2,1)}, u32[]{:S(2)}, u32[]{:S(2)}) collective-permute-start(bf16[128,2048]{1,0:T(8,128)(2,1)} %get-tuple-element.1000), channel_id=1, source_target_pairs={{0,7},{1,0},{2,1},{3,2},{4,3},{5,4},{6,5},{7,6},{8,15},{9,8},{10,9... | collective-permute-start | bytes 1572872 | tf_op jit(solution)/shard_map/ppermute | solution.py:208
  140.1 226.8 %copy-start.47 = (f32[1024]{0:T(1024)}, f32[1024]{0:T(1024)S(1)}, u32[]{:S(2)}) copy-start(f32[1024]{0:T(1024)S(1)} %convert_element_type.139) | copy-start | bytes 12292
  140.1 263.1 %copy-start.43 = (f32[1024]{0:T(1024)}, f32[1024]{0:T(1024)S(1)}, u32[]{:S(2)}) copy-start(f32[1024]{0:T(1024)S(1)} %convert_element_type.138) | copy-start | bytes 12292
  140.6 42.9 %collective-permute-start.9 = (bf16[128,2048]{1,0:T(8,128)(2,1)}, bf16[128,2048]{1,0:T(8,128)(2,1)S(1)}, u32[]{:S(2)}, u32[]{:S(2)}) collective-permute-start(bf16[128,2048]{1,0:T(8,128)(2,1)} %collective-permute-done.7), channel_id=1, source_target_pairs={{0,1},{1,2},{2,3},{3,4},{4,5},{5,6},{6,7},{7,0},{8,9},{9,10},{10,1... | collective-permute-start | bytes 1572872 | tf_op jit(solution)/shard_map/ppermute | solution.py:203
  141.2 62.7 %collective-permute-start.10 = (bf16[128,2048]{1,0:T(8,128)(2,1)}, bf16[128,2048]{1,0:T(8,128)(2,1)S(1)}, u32[]{:S(2)}, u32[]{:S(2)}) collective-permute-start(bf16[128,2048]{1,0:T(8,128)(2,1)} %collective-permute-done.8), channel_id=1, source_target_pairs={{0,7},{1,0},{2,1},{3,2},{4,3},{5,4},{6,5},{7,6},{8,15},{9,8},{10,9... | collective-permute-start | bytes 1572872 | tf_op jit(solution)/shard_map/ppermute | solution.py:208
  145.4 59.2 %collective-permute-start.2 = (bf16[128,2048]{1,0:T(8,128)(2,1)}, bf16[128,2048]{1,0:T(8,128)(2,1)S(1)}, u32[]{:S(2)}, u32[]{:S(2)}) collective-permute-start(bf16[128,2048]{1,0:T(8,128)(2,1)} %collective-permute-done), channel_id=1, source_target_pairs={{0,1},{1,2},{2,3},{3,4},{4,5},{5,6},{6,7},{7,0},{8,9},{9,10},{10,1... | collective-permute-start | bytes 1572872 | tf_op jit(solution)/shard_map/ppermute | solution.py:203
  179.7 50.5 %collective-permute-start.3 = (bf16[128,2048]{1,0:T(8,128)(2,1)}, bf16[128,2048]{1,0:T(8,128)(2,1)S(1)}, u32[]{:S(2)}, u32[]{:S(2)}) collective-permute-start(bf16[128,2048]{1,0:T(8,128)(2,1)} %collective-permute-done.1), channel_id=1, source_target_pairs={{0,7},{1,0},{2,1},{3,2},{4,3},{5,4},{6,5},{7,6},{8,15},{9,8},{10,9... | collective-permute-start | bytes 1572872 | tf_op jit(solution)/shard_map/ppermute | solution.py:208
  183.5 48.4 %collective-permute-start.11 = (bf16[128,2048]{1,0:T(8,128)(2,1)S(1)}, bf16[128,2048]{1,0:T(8,128)(2,1)S(1)}, u32[]{:S(2)}, u32[]{:S(2)}) collective-permute-start(bf16[128,2048]{1,0:T(8,128)(2,1)S(1)} %collective-permute-done.9), channel_id=1, source_target_pairs={{0,1},{1,2},{2,3},{3,4},{4,5},{5,6},{6,7},{7,0},{8,9},{9,10},{10,1... | collective-permute-start | bytes 1572872 | tf_op jit(solution)/shard_map/ppermute | solution.py:203
  204.0 54.4 %collective-permute-start.12 = (bf16[128,2048]{1,0:T(8,128)(2,1)S(1)}, bf16[128,2048]{1,0:T(8,128)(2,1)S(1)}, u32[]{:S(2)}, u32[]{:S(2)}) collective-permute-start(bf16[128,2048]{1,0:T(8,128)(2,1)S(1)} %collective-permute-done.10), channel_id=1, source_target_pairs={{0,7},{1,0},{2,1},{3,2},{4,3},{5,4},{6,5},{7,6},{8,15},{9,8},{10,9... | collective-permute-start | bytes 1572872 | tf_op jit(solution)/shard_map/ppermute | solution.py:208
  204.6 48.3 %collective-permute-start.4 = (bf16[128,2048]{1,0:T(8,128)(2,1)S(1)}, bf16[128,2048]{1,0:T(8,128)(2,1)}, u32[]{:S(2)}, u32[]{:S(2)}) collective-permute-start(bf16[128,2048]{1,0:T(8,128)(2,1)S(1)} %collective-permute-done.2), channel_id=1, source_target_pairs={{0,1},{1,2},{2,3},{3,4},{4,5},{5,6},{6,7},{7,0},{8,9},{9,10},{10,1... | collective-permute-start | bytes 1572872 | tf_op jit(solution)/shard_map/ppermute | solution.py:203
  230.2 56.0 %collective-permute-start.5 = (bf16[128,2048]{1,0:T(8,128)(2,1)S(1)}, bf16[128,2048]{1,0:T(8,128)(2,1)S(1)}, u32[]{:S(2)}, u32[]{:S(2)}) collective-permute-start(bf16[128,2048]{1,0:T(8,128)(2,1)S(1)} %collective-permute-done.3), channel_id=1, source_target_pairs={{0,7},{1,0},{2,1},{3,2},{4,3},{5,4},{6,5},{7,6},{8,15},{9,8},{10,9... | collective-permute-start | bytes 1572872 | tf_op jit(solution)/shard_map/ppermute | solution.py:208
  231.9 55.1 %collective-permute-start.13 = (bf16[128,2048]{1,0:T(8,128)(2,1)S(1)}, bf16[128,2048]{1,0:T(8,128)(2,1)S(1)}, u32[]{:S(2)}, u32[]{:S(2)}) collective-permute-start(bf16[128,2048]{1,0:T(8,128)(2,1)S(1)} %collective-permute-done.11), channel_id=1, source_target_pairs={{0,1},{1,2},{2,3},{3,4},{4,5},{5,6},{6,7},{7,0},{8,9},{9,10},{10,1... | collective-permute-start | bytes 1572872 | tf_op jit(solution)/shard_map/ppermute | solution.py:203
  252.9 68.5 %collective-permute-start.6 = (bf16[128,2048]{1,0:T(8,128)(2,1)}, bf16[128,2048]{1,0:T(8,128)(2,1)}, u32[]{:S(2)}, u32[]{:S(2)}) collective-permute-start(bf16[128,2048]{1,0:T(8,128)(2,1)} %collective-permute-done.4), channel_id=1, source_target_pairs={{0,1},{1,2},{2,3},{3,4},{4,5},{5,6},{6,7},{7,0},{8,9},{9,10},{10,1... | collective-permute-start | bytes 1572872 | tf_op jit(solution)/shard_map/ppermute | solution.py:203
  453.9 178.3 %reduce-scatter.9.cloned.1.call-start = ((), (), s32[]{:S(2)}) async-start(), calls=%async_computation.11 | async-start | bytes 4718592 | tf_op jit(solution)/shard_map/reduce_scatter | solution.py:255
  502.6 276.1 %reduce-scatter.13.cloned.1.call-start = ((), (), s32[]{:S(2)}) async-start(), calls=%async_computation.13 | async-start | bytes 4325376 | tf_op jit(solution)/shard_map/reduce_scatter | solution.py:267
  507.2 431.2 %reduce-scatter.11.cloned.1.call-start = ((), (), s32[]{:S(2)}) async-start(), calls=%async_computation.12 | async-start | bytes 12976128 | tf_op jit(solution)/shard_map/reduce_scatter | solution.py:266
  508.6 123.6 %copy-start.61 = (f32[128]{0:T(128)S(1)}, f32[128]{0:T(128)}, u32[]{:S(2)}) copy-start(f32[128]{0:T(128)} %copy-done.60) | copy-start | bytes 1540
  508.6 123.6 %copy-start.70 = (f32[128]{0:T(128)S(1)}, f32[128]{0:T(128)}, u32[]{:S(2)}) copy-start(f32[128]{0:T(128)} %copy-done.69) | copy-start | bytes 1540
  643.5 655.1 %reduce-scatter.15.cloned.1.call-start = ((), (), s32[]{:S(2)}) async-start(), calls=%async_computation.14 | async-start | bytes 17301504 | tf_op jit(solution)/shard_map/reduce_scatter | solution.py:268
  656.5 1002.3 %reduce-scatter.17.cloned.1.call-start = ((), (), s32[]{:S(2)}) async-start(), calls=%async_computation.15 | async-start | bytes 17301504 | tf_op jit(solution)/shard_map/reduce_scatter | solution.py:269
  703.8 46.6 %copy-start.20 = (f32[128,1024]{1,0:T(8,128)S(1)}, f32[128,1024]{1,0:T(8,128)}, u32[]{:S(2)}) copy-start(f32[128,1024]{1,0:T(8,128)} %copy-done.19) | copy-start | bytes 1572868
  703.8 46.6 %copy-start.22 = (f32[128,1024]{1,0:T(8,128)S(1)}, f32[128,1024]{1,0:T(8,128)}, u32[]{:S(2)}) copy-start(f32[128,1024]{1,0:T(8,128)} %copy-done.21) | copy-start | bytes 1572868
  703.8 46.6 %copy-start.86 = (f32[128]{0:T(128)S(1)}, f32[128]{0:T(128)}, u32[]{:S(2)}) copy-start(f32[128]{0:T(128)} %copy-done.85) | copy-start | bytes 1540
  703.8 46.6 %copy-start.88 = (f32[128]{0:T(128)S(1)}, f32[128]{0:T(128)}, u32[]{:S(2)}) copy-start(f32[128]{0:T(128)} %copy-done.87) | copy-start | bytes 1540
  (96 other events, 1038.1 us)
Sparse Core Ops, SparseCore 0:
  10.9 72.3 all-gather.4
  86.3 93.3 all-gather.6
  182.7 113.1 all-gather.8
  298.7 76.0 all-gather.10
  454.0 86.5 reduce-scatter.6
  544.5 87.6 reduce-scatter.8
  635.0 143.7 reduce-scatter.12
  785.4 152.9 reduce-scatter.10
  941.4 357.1 reduce-scatter.14
  1301.4 357.3 reduce-scatter.16
